TPU v7x, 512 devices: a whole 4x8x8 slice. The times are simulated.
512 devices in a mesh: section: 2 (over core), tensor: 32 (over z, x), dp: 8 (over y).
Axes of the slice: x: 4, y: 8, z: 8, core: 2. Of those that a mesh axis runs over, the one named last changes fastest.
Arguments:
- grad_out: bfloat16 [2048, 6144], P('dp', 'tensor'), may hold values from -6 to 6
- queries: bfloat16 [2, 2048, 4096], P('section', 'dp', 'tensor'), may hold values from -40 to 40
- key_rows: bfloat16 [2, 2048, 4096], P('section', 'dp', 'tensor'), may hold values from -40 to 40
- value_rows: bfloat16 [2, 2048, 4096], P('section', 'dp', 'tensor'), may hold values from -6 to 6
- w_qkv: bfloat16 [2, 6144, 12288], P('section', 'dp', 'tensor'), may hold values from -0.078125 to 0.078125
- w_out: bfloat16 [2, 4096, 6144], P('section', 'tensor', 'dp'), may hold values from -0.09375 to 0.09375
- seg_lengths: int32 [8, 3], P('dp'), may hold values from 0 to 128, as said below
Outputs:
- input_grad: bfloat16 [2, 2048, 6144], P('section', 'dp', 'tensor')
- out_weight_grad: bfloat16 [2, 4096, 6144], P('section', 'tensor', 'dp')
Inputs may be any that keep to these rules, and one draw needn't show every extreme that they name: `seg_lengths`: each row sums to 256, holds one image of exactly 128 patches and either a second of 128 patches and an empty last slot, or two of 64 patches.
All inputs are finite; a program needn't handle non-finite values.
Results may differ from a plain program's by a relative error of at most 0.023.
Values may be sent and summed in bfloat16 or wider, within the bound.
A program may use at most 64 MiB of HBM per device.

v0:
```python
import jax
import jax.numpy as jnp
from jax import lax
from jax.sharding import PartitionSpec as P

PACK = 256
MB = 1
negative_big = -1e30


def passed_along(value, axis, steps):
    count = lax.axis_size(axis)
    first, last = (max(0, -steps), min(count, count - steps))
    return lax.ppermute(value, axis, [(source, source + steps) for source in range(first, last)])


def contract(left, right, left_dim, right_dim):
    return lax.dot_general(
        left, right, (((left_dim,), (right_dim,)), ((), ())), preferred_element_type=jnp.float32
    )


def attend_back(query_blk, key_blk, value_blk, grad_attn, same_seg, scaling):
    scores = contract(query_blk, key_blk, 1, 1) * scaling
    scores = jnp.where(same_seg, scores, negative_big)
    peak = jnp.max(scores, axis=-1, keepdims=True)
    shifted = jnp.exp(scores - peak)
    probs = shifted / jnp.sum(shifted, axis=-1, keepdims=True)
    probs_low = probs.astype(jnp.bfloat16)
    attended = jnp.dot(probs_low, value_blk, preferred_element_type=jnp.float32).astype(
        jnp.bfloat16
    )
    grad_value = contract(probs_low, grad_attn, 0, 0).astype(jnp.bfloat16)
    grad_probs = contract(grad_attn, value_blk, 1, 1)
    centred = jnp.sum(probs * grad_probs, axis=-1, keepdims=True)
    grad_scores = (probs * (grad_probs - centred) * scaling).astype(jnp.bfloat16)
    grad_query = jnp.dot(grad_scores, key_blk, preferred_element_type=jnp.float32).astype(
        jnp.bfloat16
    )
    grad_key = contract(grad_scores, query_blk, 0, 0).astype(jnp.bfloat16)
    return (attended, grad_query, grad_key, grad_value)


def per_device(grad_out, queries, key_rows, value_rows, w_qkv, w_out, seg_lengths):
    sections = lax.axis_size("section")
    section_index = lax.axis_index("section")
    head_index = lax.axis_index("tensor")
    width = grad_out.shape[1]
    qkv_full, out_full = (
        lax.all_gather(w_qkv, "dp", axis=1, tiled=True),
        lax.all_gather(w_out, "dp", axis=2, tiled=True),
    )
    proj_in = qkv_full[0]
    proj_out = out_full[0]
    head_dim = proj_out.shape[0]
    full_width = proj_out.shape[1]
    scaling = head_dim ** (-0.5)
    seg_ends = jnp.cumsum(seg_lengths, axis=1)
    position = jnp.arange(PACK, dtype=jnp.int32)
    seg_table = jnp.sum((position[None, :, None] >= seg_ends[:, None, :]).astype(jnp.int32), axis=2)
    offset = sections - 1 - section_index
    carried = jnp.zeros((PACK, width), jnp.bfloat16)
    result = jnp.zeros((MB * PACK, width), jnp.bfloat16)
    grad_acc = jnp.zeros((head_dim, full_width), jnp.float32)
    for step_index in range(MB + sections - 1):
        micro = step_index - offset
        active = (micro >= 0) & (micro < MB)
        which = jnp.clip(micro, 0, MB - 1)
        incoming = jnp.where(section_index == sections - 1, grad_out, carried)
        whole = lax.all_gather(incoming, "tensor", axis=1, tiled=True)
        query_blk = queries[0]
        key_blk = key_rows[0]
        value_blk = value_rows[0]
        seg_ids = lax.dynamic_index_in_dim(seg_table, which, 0, keepdims=False)
        same_seg = seg_ids[:, None] == seg_ids[None, :]
        grad_attn = contract(whole, proj_out, 1, 1).astype(jnp.bfloat16)
        attended, grad_query, grad_key, grad_value = attend_back(
            query_blk, key_blk, value_blk, grad_attn, same_seg, scaling
        )
        combined = jnp.concatenate([grad_query, grad_key, grad_value], axis=1)
        head_term = contract(combined, proj_in, 1, 1)
        summed = lax.psum(head_term.astype(jnp.bfloat16), "tensor").astype(jnp.float32)
        share = lax.dynamic_slice_in_dim(summed, head_index * width, width, 1)
        block_grad = (incoming.astype(jnp.float32) + share).astype(jnp.bfloat16)
        result = jnp.where(active, block_grad, result)
        grad_acc = grad_acc + jnp.where(active, contract(attended, whole, 0, 0), 0.0)
        carried = passed_along(block_grad, "section", -1)
    weight_share = lax.psum_scatter(
        grad_acc.astype(jnp.bfloat16), "dp", scatter_dimension=1, tiled=True
    )
    return (result[None], weight_share[None])


def solution(mesh):
    return jax.shard_map(
        per_device,
        mesh=mesh,
        in_specs=(
            P("dp", "tensor"),
            P("section", "dp", "tensor"),
            P("section", "dp", "tensor"),
            P("section", "dp", "tensor"),
            P("section", "dp", "tensor"),
            P("section", "tensor", "dp"),
            P("dp", None),
        ),
        out_specs=(P("section", "dp", "tensor"), P("section", "tensor", "dp")),
        check_vma=False,
    )
```

profile of v0, /device:TPU:6, one launch (start us, length us, event | category | flops | bytes accessed | tf_op | source)
XLA Modules:
  0.0 695.8 jit_solution(12003352529557310799)
XLA Ops:
  7.2 0.0 copy-start
  7.2 0.0 all-gather.7.cloned.1.call-start
  7.2 0.7 all-gather.7.cloned.1.call-update
  7.9 0.0 all-gather.5.cloned.1.call-start
  8.0 0.7 broadcast_select_fusion.1
  8.6 0.0 all-gather.5.cloned.1.call-update
  8.7 0.0 all-gather.9.cloned.1.call-start
  8.7 0.7 all-gather.9.cloned.1.call-update
  9.4 0.0 all-reduce.3.cloned.1.call-start
  9.4 0.8 reduce_window_sum.11
  10.3 0.1 fusion.40
  10.4 1.1 fusion.49
  11.5 0.1 fusion.16
  11.5 0.0 copy-start.8
  11.5 0.0 copy-start.9
  11.5 45.2 %all-gather.7.cloned.1.call-done = bf16[1,128,6144]{2,1,0:T(8,128)(2,1)} async-done(((bf16[1,128,768]{2,1,0:T(8,128)(2,1)}), bf16[1,128,6144]{2,1,0:T(8,128)(2,1)}) %all-gather.7.cloned.1.call-update) | async-done | bytes 1572880 | tf_op jit(solution)/shard_map/all_gather | solution.py:51
  56.7 86.7 %all-gather.5.cloned.1.call-done = bf16[256,6144]{0,1:T(8,128)(2,1)} async-done(((bf16[256,192]{0,1:T(8,128)(2,1)}), bf16[256,6144]{0,1:T(8,128)(2,1)}) %all-gather.5.cloned.1.call-update) | async-done | bytes 3145744 | tf_op jit(solution)/shard_map/all_gather | solution.py:70
  143.4 3.4 fusion.9
  146.8 0.0 copy-done
  146.8 0.2 multiply_reduce_fusion.1
  147.1 0.1 multiply_convert_fusion.1
  147.1 0.0 copy-done.8
  147.1 0.2 convolution_convert_fusion.7
  147.3 0.0 copy-done.9
  147.3 0.2 convolution_convert_fusion.8
  147.6 0.2 convolution_convert_fusion.6
  147.7 57.7 %all-gather.9.cloned.1.call-done = bf16[1,6144,384]{2,1,0:T(8,128)(2,1)} async-done(((bf16[1,768,384]{2,1,0:T(8,128)(2,1)}), bf16[1,6144,384]{2,1,0:T(8,128)(2,1)}) %all-gather.9.cloned.1.call-update) | async-done | bytes 4718608 | tf_op jit(solution)/shard_map/all_gather | solution.py:50
  205.5 5.9 convolution_convert_fusion.1
  211.4 0.0 copy-start.4
  211.4 0.0 copy-start.3
  211.4 0.0 all-reduce.3.cloned.1.call-update
  211.4 0.0 all-gather.11.cloned.1.call-start
  211.5 168.1 %all-reduce.3.cloned.1.call-done = bf16[256,6144]{0,1:T(8,128)(2,1)} async-done(((bf16[256,6144]{0,1:T(8,128)(2,1)}), bf16[256,6144]{0,1:T(8,128)(2,1)}) %all-reduce.3.cloned.1.call-update) | async-done | bytes 3145744 | tf_op jit(solution)/shard_map/psum | solution.py:82
  379.6 0.0 copy-done.4
  379.6 0.9 add_convert_fusion.1
  380.5 0.0 copy-start.6
  380.5 1.3 collective-permute-start
  381.8 1.9 collective-permute-done
  383.7 0.7 broadcast_select_fusion
  384.4 0.0 all-gather.11.cloned.1.call-update
  384.4 0.0 all-reduce.5.cloned.1.call-start
  384.4 82.7 %all-gather.11.cloned.1.call-done = bf16[256,6144]{0,1:T(8,128)(2,1)} async-done(((bf16[256,192]{0,1:T(8,128)(2,1)}), bf16[256,6144]{0,1:T(8,128)(2,1)}) %all-gather.11.cloned.1.call-update) | async-done | bytes 3145744 | tf_op jit(solution)/shard_map/all_gather | solution.py:70
  467.2 0.0 copy-done.3
  467.2 2.9 fusion.12
  470.1 0.2 convolution_convert_fusion.3
  470.3 0.2 multiply_reduce_fusion
  470.5 0.0 copy-done.6
  470.5 0.1 multiply_convert_fusion
  470.6 0.2 convolution_convert_fusion.4
  470.8 0.2 convolution_convert_fusion.5
  471.0 5.9 convolution_convert_fusion
  477.0 0.0 all-reduce.5.cloned.1.call-update
  477.0 0.0 reduce-scatter.2.cloned.1.call-start
  477.0 0.2 convolution_convert_fusion.2
  477.3 1.6 copy-done.1
  478.8 1.2 convolution_select_fusion.1
  480.0 0.7 copy-done.2
  480.7 2.3 fusion.1
  483.1 0.0 reduce-scatter.2.cloned.1.call-update
  483.1 160.8 %all-reduce.5.cloned.1.call-done = bf16[256,6144]{0,1:T(8,128)(2,1)} async-done(((bf16[256,6144]{0,1:T(8,128)(2,1)}), bf16[256,6144]{0,1:T(8,128)(2,1)}) %all-reduce.5.cloned.1.call-update) | async-done | bytes 3145744 | tf_op jit(solution)/shard_map/psum | solution.py:82
  644.0 0.0 copy-done.5
  644.0 0.0 copy-done.7
  644.0 1.6 fusion.28
  645.5 43.4 %reduce-scatter.2.cloned.1.call-done = bf16[128,768]{1,0:T(8,128)(2,1)} async-done(((bf16[128,6144]{1,0:T(8,128)(2,1)}), bf16[128,768]{1,0:T(8,128)(2,1)}) %reduce-scatter.2.cloned.1.call-update) | async-done | bytes 196624 | tf_op jit(solution)/shard_map/reduce_scatter | solution.py:88
  (4 shorter events, 0.0 us)
Async XLA Ops:
  7.2 139.7 %copy-start = (bf16[1,256,128]{2,1,0:T(8,128)(2,1)S(1)}, bf16[1,256,128]{2,1,0:T(8,128)(2,1)}, u32[]{:S(2)}) copy-start(bf16[1,256,128]{2,1,0:T(8,128)(2,1)} %param.10) | copy-start | bytes 196612
  7.2 49.5 %all-gather.7.cloned.1.call-start = ((), (), s32[]{:S(2)}) async-start(), calls=%async_computation.2 | async-start | bytes 1769472 | tf_op jit(solution)/shard_map/all_gather | solution.py:51
  7.9 135.5 %all-gather.5.cloned.1.call-start = ((), (), s32[]{:S(2)}) async-start(), calls=%async_computation.1 | async-start | bytes 3244032 | tf_op jit(solution)/shard_map/all_gather | solution.py:70
  8.7 196.8 %all-gather.9.cloned.1.call-start = ((), (), s32[]{:S(2)}) async-start(), calls=%async_computation.3 | async-start | bytes 5308416 | tf_op jit(solution)/shard_map/all_gather | solution.py:50
  9.4 370.2 %all-reduce.3.cloned.1.call-start = ((), (), s32[]{:S(2)}) async-start(), calls=%async_computation.4 | async-start | bytes 6291456 | tf_op jit(solution)/shard_map/psum | solution.py:82
  11.5 135.6 %copy-start.8 = (bf16[1,256,128]{2,1,0:T(8,128)(2,1)S(1)}, bf16[1,256,128]{2,1,0:T(8,128)(2,1)}, u32[]{:S(2)}) copy-start(bf16[1,256,128]{2,1,0:T(8,128)(2,1)} %param.8) | copy-start | bytes 196612
  11.5 135.8 %copy-start.9 = (bf16[1,256,128]{2,1,0:T(8,128)(2,1)S(1)}, bf16[1,256,128]{2,1,0:T(8,128)(2,1)}, u32[]{:S(2)}) copy-start(bf16[1,256,128]{2,1,0:T(8,128)(2,1)} %param.9) | copy-start | bytes 196612
  211.4 168.2 %copy-start.4 = (bf16[256,192]{0,1:T(8,128)(2,1)S(1)}, bf16[256,192]{0,1:T(8,128)(2,1)}, u32[]{:S(2)}) copy-start(bf16[256,192]{0,1:T(8,128)(2,1)} %param.7) | copy-start | bytes 294916
  211.4 255.8 %copy-start.3 = (bf16[1,128,6144]{2,1,0:T(8,128)(2,1)S(1)}, bf16[1,128,6144]{2,1,0:T(8,128)(2,1)}, u32[]{:S(2)}) copy-start(bf16[1,128,6144]{2,1,0:T(8,128)(2,1)} %all-gather.7.cloned.1.call-done) | copy-start | bytes 4718596
  211.4 255.8 %all-gather.11.cloned.1.call-start = ((), (), s32[]{:S(2)}) async-start(), calls=%async_computation.5 | async-start | bytes 3244032 | tf_op jit(solution)/shard_map/all_gather | solution.py:70
  380.5 90.0 %copy-start.6 = (bf16[256,192]{0,1:T(8,128)(2,1)}, bf16[256,192]{0,1:T(8,128)(2,1)S(1)}, u32[]{:S(2)}) copy-start(bf16[256,192]{0,1:T(8,128)(2,1)S(1)} %add_convert_fusion.1) | copy-start | bytes 294916
  380.5 3.2 collective-permute-start
  384.4 259.6 %all-reduce.5.cloned.1.call-start = ((), (), s32[]{:S(2)}) async-start(), calls=%async_computation.6 | async-start | bytes 6291456 | tf_op jit(solution)/shard_map/psum | solution.py:82
  477.0 1.9 copy-start.1
  477.0 212.0 %reduce-scatter.2.cloned.1.call-start = ((), (), s32[]{:S(2)}) async-start(), calls=%async_computation.7 | async-start | bytes 1769472 | tf_op jit(solution)/shard_map/reduce_scatter | solution.py:88
  478.8 1.9 copy-start.2
  480.7 163.2 %copy-start.5 = (bf16[256,192]{0,1:T(8,128)(2,1)S(1)}, bf16[256,192]{0,1:T(8,128)(2,1)}, u32[]{:S(2)}) copy-start(bf16[256,192]{0,1:T(8,128)(2,1)} %broadcast_select_fusion) | copy-start | bytes 294916
  480.7 163.2 %copy-start.7 = (bf16[256,192]{0,1:T(8,128)(2,1)S(1)}, bf16[256,192]{0,1:T(8,128)(2,1)}, u32[]{:S(2)}) copy-start(bf16[256,192]{0,1:T(8,128)(2,1)} %copy-done.6) | copy-start | bytes 294916
Sparse Core Ops, SparseCore 0:
  10.1 46.5 all-gather.6
  60.4 82.9 all-gather.4
  145.5 59.8 all-gather.8
  211.5 167.9 all-reduce.2
  384.5 82.6 all-gather.10
  477.1 166.8 all-reduce.4
  647.4 41.5 reduce-scatter.1
where the time goes:
time: 696 us
  waiting for transfers between devices  648 us (93%)
  matrix products  24.6 us (4%)
  between operations  14.3 us (2%)
    psum x2, waiting for transfers between devices, per_device(): lax.psum(head_term.astype(jnp.bfloat16), 'tensor').astype(jnp.float32)  329 us
    all_gather x2, waiting for transfers between devices, per_device(): whole = lax.all_gather(incoming, 'tensor', axis=1, tiled=True)  169 us
    all_gather x1, waiting for transfers between devices, per_device(): lax.all_gather(w_qkv, 'dp', axis=1, tiled=True)  57.7 us
    all_gather x1, waiting for transfers between devices, per_device(): lax.all_gather(w_out, 'dp', axis=2, tiled=True)  45.2 us
    reduce_scatter x1, waiting for transfers between devices, per_device(): lax.psum_scatter(grad_acc.astype(jnp.bfloat16), 'dp', scatter_dimension=1...  43.4 us
    dot_general x13, matrix products, contract(): lax.dot_general(left, right, (((left_dim,), (right_dim,)), ((), ())), pre...  23.9 us
  transfers between devices with their start and end apart: 8, of which 8 were waited for; matrix products, arithmetic and copies ran while one was open for 2% of the time, Pallas kernels for 0%

commit v1 on v0

--- a/solution.py
+++ b/solution.py
@@ -46,10 +46,34 @@
     section_index = lax.axis_index("section")
     head_index = lax.axis_index("tensor")
     width = grad_out.shape[1]
-    qkv_full, out_full = (
-        lax.all_gather(w_qkv, "dp", axis=1, tiled=True),
-        lax.all_gather(w_out, "dp", axis=2, tiled=True),
-    )
+
+    def _serve_plane(inputs, dim_at):
+        arr_next = lax.axis_size("dp")
+        n_now = lax.axis_index("dp")
+        right_arr, step_out, field_out = (arr_next, n_now, inputs.shape[dim_at])
+        made = [j * right_arr if hop_no == dim_at else j for hop_no, j in enumerate(inputs.shape)]
+        z = jnp.zeros(made, inputs.dtype)
+        y = current_value = inputs
+        view_out = lax.dynamic_update_slice_in_dim(z, inputs, step_out * field_out, axis=dim_at)
+        for dd in range(1, right_arr // 2 + 1):
+            piece_now = range(right_arr)
+            w_next = map(lambda hop_no: (hop_no, (hop_no + 1) % right_arr), piece_now)
+            shaped = list(w_next)
+            y = lax.ppermute(y, "dp", shaped)
+            view_out = lax.dynamic_update_slice_in_dim(
+                view_out, y, (step_out - dd) % right_arr * field_out, axis=dim_at
+            )
+            if 2 * dd < right_arr:
+                kept_arr = range(right_arr)
+                main = map(lambda hop_no: (hop_no, (hop_no - 1) % right_arr), kept_arr)
+                prior = list(main)
+                current_value = lax.ppermute(current_value, "dp", prior)
+                view_out = lax.dynamic_update_slice_in_dim(
+                    view_out, current_value, (step_out + dd) % right_arr * field_out, axis=dim_at
+                )
+        return view_out
+
+    qkv_full, out_full = (lax.all_gather(w_qkv, "dp", axis=1, tiled=True), _serve_plane(w_out, 2))
     proj_in = qkv_full[0]
     proj_out = out_full[0]
     head_dim = proj_out.shape[0]

time: 696 us -> 653 us (0.938)
  waiting for transfers between devices: 648 us -> 581 us
  starting transfers between devices: 1.57 us -> 24.8 us
    all_gather x1 -> x0, waiting for transfers between devices: 45.2 us -> none  [per_device(): lax.all_gather(w_out, 'dp', axis=2, tiled=True)]
    all_gather x2, waiting for transfers between devices: 169 us -> 135 us  [per_device(): whole = lax.all_gather(incoming, 'tensor', axis=1, tiled=True)]
    ppermute x0 -> x7, starting transfers between devices: none -> 23.3 us  [the longest x3 14.1 us: _serve_plane(): current_value = lax.ppermute(current_value, 'dp', prior)]
    ppermute x0 -> x7, waiting for transfers between devices: none -> 13.2 us  [the longest x4 13.2 us: _serve_plane(): y = lax.ppermute(y, 'dp', shaped)]
  transfers between devices with their start and end apart: 8 -> 14, of which waited for: 8 -> 11; matrix products, arithmetic and copies ran while one was open for 2% -> 2% of each run, Pallas kernels for 0% -> 0%
where the time goes in v1:
time: 653 us; the launch traced here: 652 us
  waiting for transfers between devices  581 us (89%)
  starting transfers between devices  24.8 us (4%)
  matrix products  24 us (4%)
  between operations  14.6 us (2%)
    psum x2, waiting for transfers between devices, per_device(): lax.psum(head_term.astype(jnp.bfloat16), 'tensor').astype(jnp.float32)  329 us
    all_gather x2, waiting for transfers between devices, per_device(): whole = lax.all_gather(incoming, 'tensor', axis=1, tiled=True)  135 us
    all_gather x1, waiting for transfers between devices, per_device(): lax.all_gather(w_qkv, 'dp', axis=1, tiled=True)  58.2 us
    reduce_scatter x1, waiting for transfers between devices, per_device(): lax.psum_scatter(grad_acc.astype(jnp.bfloat16), 'dp', scatter_dimension=1...  43.3 us
    dot_general x13, matrix products, contract(): lax.dot_general(left, right, (((left_dim,), (right_dim,)), ((), ())), pre...  23.3 us
    ppermute x3, starting transfers between devices, _serve_plane(): current_value = lax.ppermute(current_value, 'dp', prior)  14.1 us
    ppermute x4, waiting for transfers between devices, _serve_plane(): y = lax.ppermute(y, 'dp', shaped)  13.2 us
  transfers between devices with their start and end apart: 14, of which 11 were waited for; matrix products, arithmetic and copies ran while one was open for 2% of the time, Pallas kernels for 0%

profile of v1, /device:TPU:6, one launch (start us, length us, event | category | flops | bytes accessed | tf_op | source)
XLA Modules:
  0.0 652.5 jit_solution(17170259759607919953)
XLA Ops:
  7.2 0.0 copy-start
  7.2 0.0 copy-start.9
  7.2 0.0 all-gather.4.cloned.1.call-start
  7.2 0.7 broadcast_select_fusion.1
  7.9 0.0 all-gather.4.cloned.1.call-update
  7.9 0.0 all-gather.6.cloned.1.call-start
  8.0 0.7 all-gather.6.cloned.1.call-update
  8.7 0.0 all-reduce.3.cloned.1.call-start
  8.7 3.5 collective-permute-start
  12.2 3.8 collective-permute-start.1
  16.2 0.8 reduce_window_sum.11
  17.0 0.1 fusion.30
  17.1 1.1 fusion.39
  18.2 0.1 fusion.6
  18.3 0.1 squeeze.39
  18.4 1.5 collective-permute-done
  20.0 1.9 collective-permute-start.2
  21.9 5.1 collective-permute-start.3
  27.1 2.9 collective-permute-done.2
  30.0 1.9 collective-permute-start.4
  31.9 0.0 collective-permute-done.3
  31.9 5.1 collective-permute-start.5
  37.1 2.0 collective-permute-done.4
  39.1 1.9 collective-permute-start.6
  41.1 6.8 %collective-permute-done.6 = bf16[1,128,768]{2,1,0:T(8,128)(2,1)S(1)} collective-permute-done((bf16[1,128,768]{2,1,0:T(8,128)(2,1)S(1)}, bf16[1,128,768]{2,1,0:T(8,128)(2,1)S(1)}, u32[]{:S(2)}, u32[]{:S(2)}) %collective-permute-start.6) | collective-permute-done | bytes 196640 | tf_op jit(solution)/shard_map/ppermute | solution.py:62
  47.9 0.0 copy-start.7
  47.9 0.0 copy-start.8
  48.0 52.4 %all-gather.4.cloned.1.call-done = bf16[256,6144]{0,1:T(8,128)(2,1)} async-done(((bf16[256,192]{0,1:T(8,128)(2,1)}), bf16[256,6144]{0,1:T(8,128)(2,1)}) %all-gather.4.cloned.1.call-update) | async-done | bytes 3145744 | tf_op jit(solution)/shard_map/all_gather | solution.py:94
  100.4 2.9 convolution_convert_fusion.3
  103.3 0.2 multiply_reduce_fusion.1
  103.5 0.1 multiply_convert_fusion.1
  103.6 0.2 convolution_convert_fusion.9
  103.8 0.2 convolution_convert_fusion.10
  104.0 0.2 convolution_convert_fusion.8
  104.2 58.2 %all-gather.6.cloned.1.call-done = bf16[1,6144,384]{2,1,0:T(8,128)(2,1)} async-done(((bf16[1,768,384]{2,1,0:T(8,128)(2,1)}), bf16[1,6144,384]{2,1,0:T(8,128)(2,1)}) %all-gather.6.cloned.1.call-update) | async-done | bytes 4718608 | tf_op jit(solution)/shard_map/all_gather | solution.py:76
  162.4 5.9 convolution_convert_fusion.1
  168.3 0.0 all-reduce.3.cloned.1.call-update
  168.4 0.0 all-gather.8.cloned.1.call-start
  168.4 168.1 %all-reduce.3.cloned.1.call-done = bf16[256,6144]{0,1:T(8,128)(2,1)} async-done(((bf16[256,6144]{0,1:T(8,128)(2,1)}), bf16[256,6144]{0,1:T(8,128)(2,1)}) %all-reduce.3.cloned.1.call-update) | async-done | bytes 3145744 | tf_op jit(solution)/shard_map/psum | solution.py:106
  336.5 0.9 add_convert_fusion.1
  337.4 1.3 collective-permute-start.7
  338.7 1.9 collective-permute-done.7
  340.6 0.7 broadcast_select_fusion
  341.3 0.0 all-gather.8.cloned.1.call-update
  341.3 0.0 all-reduce.5.cloned.1.call-start
  341.3 82.7 %all-gather.8.cloned.1.call-done = bf16[256,6144]{0,1:T(8,128)(2,1)} async-done(((bf16[256,192]{0,1:T(8,128)(2,1)}), bf16[256,6144]{0,1:T(8,128)(2,1)}) %all-gather.8.cloned.1.call-update) | async-done | bytes 3145744 | tf_op jit(solution)/shard_map/all_gather | solution.py:94
  424.1 2.9 convolution_convert_fusion.2
  427.0 0.2 convolution_convert_fusion.5
  427.2 0.2 multiply_reduce_fusion
  427.4 0.1 multiply_convert_fusion
  427.5 0.2 convolution_convert_fusion.6
  427.7 0.2 convolution_convert_fusion.7
  427.9 5.9 convolution_convert_fusion
  433.8 0.0 all-reduce.5.cloned.1.call-update
  433.8 0.0 reduce-scatter.2.cloned.1.call-start
  433.9 0.2 convolution_convert_fusion.4
  434.2 1.6 copy-done.1
  435.7 1.2 convolution_select_fusion.1
  436.9 0.7 copy-done.2
  437.6 2.3 fusion.1
  439.9 0.0 reduce-scatter.2.cloned.1.call-update
  439.9 160.9 %all-reduce.5.cloned.1.call-done = bf16[256,6144]{0,1:T(8,128)(2,1)} async-done(((bf16[256,6144]{0,1:T(8,128)(2,1)}), bf16[256,6144]{0,1:T(8,128)(2,1)}) %all-reduce.5.cloned.1.call-update) | async-done | bytes 3145744 | tf_op jit(solution)/shard_map/psum | solution.py:106
  600.8 1.6 fusion.18
  602.4 43.3 %reduce-scatter.2.cloned.1.call-done = bf16[128,768]{1,0:T(8,128)(2,1)} async-done(((bf16[128,6144]{1,0:T(8,128)(2,1)}), bf16[128,768]{1,0:T(8,128)(2,1)}) %reduce-scatter.2.cloned.1.call-update) | async-done | bytes 196624 | tf_op jit(solution)/shard_map/reduce_scatter | solution.py:112
  (24 shorter events, 0.2 us)
Async XLA Ops:
  7.2 96.1 %copy-start = (bf16[1,256,128]{2,1,0:T(8,128)(2,1)S(1)}, bf16[1,256,128]{2,1,0:T(8,128)(2,1)}, u32[]{:S(2)}) copy-start(bf16[1,256,128]{2,1,0:T(8,128)(2,1)} %param.10) | copy-start | bytes 196612
  7.2 11.2 %copy-start.9 = (bf16[1,128,768]{2,1,0:T(8,128)(2,1)S(1)}, bf16[1,128,768]{2,1,0:T(8,128)(2,1)}, u32[]{:S(2)}) copy-start(bf16[1,128,768]{2,1,0:T(8,128)(2,1)} %param.12) | copy-start | bytes 589828
  7.2 93.2 %all-gather.4.cloned.1.call-start = ((), (), s32[]{:S(2)}) async-start(), calls=%async_computation.1 | async-start | bytes 3244032 | tf_op jit(solution)/shard_map/all_gather | solution.py:94
  7.9 154.5 %all-gather.6.cloned.1.call-start = ((), (), s32[]{:S(2)}) async-start(), calls=%async_computation.2 | async-start | bytes 5308416 | tf_op jit(solution)/shard_map/all_gather | solution.py:76
  8.7 327.8 %all-reduce.3.cloned.1.call-start = ((), (), s32[]{:S(2)}) async-start(), calls=%async_computation.3 | async-start | bytes 6291456 | tf_op jit(solution)/shard_map/psum | solution.py:106
  8.7 11.2 %collective-permute-start = (bf16[1,128,768]{2,1,0:T(8,128)(2,1)}, bf16[1,128,768]{2,1,0:T(8,128)(2,1)S(1)}, u32[]{:S(2)}, u32[]{:S(2)}) collective-permute-start(bf16[1,128,768]{2,1,0:T(8,128)(2,1)} %param.12), channel_id=1, source_target_pairs={{0,1},{1,2},{2,3},{3,4},{4,5},{5,6},{6,7},{7,0},{8,9},{9,10},{10,1... | collective-permute-start | bytes 589832 | tf_op jit(solution)/shard_map/ppermute | solution.py:62
  12.2 9.7 %collective-permute-start.1 = (bf16[1,128,768]{2,1,0:T(8,128)(2,1)}, bf16[1,128,768]{2,1,0:T(8,128)(2,1)S(1)}, u32[]{:S(2)}, u32[]{:S(2)}) collective-permute-start(bf16[1,128,768]{2,1,0:T(8,128)(2,1)} %param.12), channel_id=1, source_target_pairs={{0,7},{1,0},{2,1},{3,2},{4,3},{5,4},{6,5},{7,6},{8,15},{9,8},{10,9... | collective-permute-start | bytes 589832 | tf_op jit(solution)/shard_map/ppermute | solution.py:70
  20.0 10.0 %collective-permute-start.2 = (bf16[1,128,768]{2,1,0:T(8,128)(2,1)S(1)}, bf16[1,128,768]{2,1,0:T(8,128)(2,1)S(1)}, u32[]{:S(2)}, u32[]{:S(2)}) collective-permute-start(bf16[1,128,768]{2,1,0:T(8,128)(2,1)S(1)} %collective-permute-done), channel_id=1, source_target_pairs={{0,1},{1,2},{2,3},{3,4},{4,5},{5,6},{6,7},{7,0},{8,9},{9,10},{10,1... | collective-permute-start | bytes 589832 | tf_op jit(solution)/shard_map/ppermute | solution.py:62
  21.9 10.0 %collective-permute-start.3 = (bf16[1,128,768]{2,1,0:T(8,128)(2,1)S(1)}, bf16[1,128,768]{2,1,0:T(8,128)(2,1)S(1)}, u32[]{:S(2)}, u32[]{:S(2)}) collective-permute-start(bf16[1,128,768]{2,1,0:T(8,128)(2,1)S(1)} %collective-permute-done.1), channel_id=1, source_target_pairs={{0,7},{1,0},{2,1},{3,2},{4,3},{5,4},{6,5},{7,6},{8,15},{9,8},{10,9... | collective-permute-start | bytes 589832 | tf_op jit(solution)/shard_map/ppermute | solution.py:70
  30.0 9.2 %collective-permute-start.4 = (bf16[1,128,768]{2,1,0:T(8,128)(2,1)S(1)}, bf16[1,128,768]{2,1,0:T(8,128)(2,1)S(1)}, u32[]{:S(2)}, u32[]{:S(2)}) collective-permute-start(bf16[1,128,768]{2,1,0:T(8,128)(2,1)S(1)} %collective-permute-done.2), channel_id=1, source_target_pairs={{0,1},{1,2},{2,3},{3,4},{4,5},{5,6},{6,7},{7,0},{8,9},{9,10},{10,1... | collective-permute-start | bytes 589832 | tf_op jit(solution)/shard_map/ppermute | solution.py:62
  31.9 9.2 %collective-permute-start.5 = (bf16[1,128,768]{2,1,0:T(8,128)(2,1)S(1)}, bf16[1,128,768]{2,1,0:T(8,128)(2,1)S(1)}, u32[]{:S(2)}, u32[]{:S(2)}) collective-permute-start(bf16[1,128,768]{2,1,0:T(8,128)(2,1)S(1)} %collective-permute-done.3), channel_id=1, source_target_pairs={{0,7},{1,0},{2,1},{3,2},{4,3},{5,4},{6,5},{7,6},{8,15},{9,8},{10,9... | collective-permute-start | bytes 589832 | tf_op jit(solution)/shard_map/ppermute | solution.py:70
  39.1 8.8 %collective-permute-start.6 = (bf16[1,128,768]{2,1,0:T(8,128)(2,1)S(1)}, bf16[1,128,768]{2,1,0:T(8,128)(2,1)S(1)}, u32[]{:S(2)}, u32[]{:S(2)}) collective-permute-start(bf16[1,128,768]{2,1,0:T(8,128)(2,1)S(1)} %collective-permute-done.4), channel_id=1, source_target_pairs={{0,1},{1,2},{2,3},{3,4},{4,5},{5,6},{6,7},{7,0},{8,9},{9,10},{10,1... | collective-permute-start | bytes 589832 | tf_op jit(solution)/shard_map/ppermute | solution.py:62
  47.9 55.7 %copy-start.7 = (bf16[1,256,128]{2,1,0:T(8,128)(2,1)S(1)}, bf16[1,256,128]{2,1,0:T(8,128)(2,1)}, u32[]{:S(2)}) copy-start(bf16[1,256,128]{2,1,0:T(8,128)(2,1)} %param.8) | copy-start | bytes 196612
  47.9 55.9 %copy-start.8 = (bf16[1,256,128]{2,1,0:T(8,128)(2,1)S(1)}, bf16[1,256,128]{2,1,0:T(8,128)(2,1)}, u32[]{:S(2)}) copy-start(bf16[1,256,128]{2,1,0:T(8,128)(2,1)} %param.9) | copy-start | bytes 196612
  168.3 168.1 %copy-start.3 = (bf16[256,192]{0,1:T(8,128)(2,1)S(1)}, bf16[256,192]{0,1:T(8,128)(2,1)}, u32[]{:S(2)}) copy-start(bf16[256,192]{0,1:T(8,128)(2,1)} %param.7) | copy-start | bytes 294916
  168.4 255.7 %all-gather.8.cloned.1.call-start = ((), (), s32[]{:S(2)}) async-start(), calls=%async_computation.4 | async-start | bytes 3244032 | tf_op jit(solution)/shard_map/all_gather | solution.py:94
  337.4 90.0 %copy-start.5 = (bf16[256,192]{0,1:T(8,128)(2,1)}, bf16[256,192]{0,1:T(8,128)(2,1)S(1)}, u32[]{:S(2)}) copy-start(bf16[256,192]{0,1:T(8,128)(2,1)S(1)} %add_convert_fusion.1) | copy-start | bytes 294916
  337.4 3.2 collective-permute-start.7
  341.3 259.5 %all-reduce.5.cloned.1.call-start = ((), (), s32[]{:S(2)}) async-start(), calls=%async_computation.5 | async-start | bytes 6291456 | tf_op jit(solution)/shard_map/psum | solution.py:106
  433.8 1.9 copy-start.1
  433.8 211.8 %reduce-scatter.2.cloned.1.call-start = ((), (), s32[]{:S(2)}) async-start(), calls=%async_computation.6 | async-start | bytes 1769472 | tf_op jit(solution)/shard_map/reduce_scatter | solution.py:112
  435.7 1.9 copy-start.2
  437.6 163.2 %copy-start.4 = (bf16[256,192]{0,1:T(8,128)(2,1)S(1)}, bf16[256,192]{0,1:T(8,128)(2,1)}, u32[]{:S(2)}) copy-start(bf16[256,192]{0,1:T(8,128)(2,1)} %broadcast_select_fusion) | copy-start | bytes 294916
  437.6 163.2 %copy-start.6 = (bf16[256,192]{0,1:T(8,128)(2,1)S(1)}, bf16[256,192]{0,1:T(8,128)(2,1)}, u32[]{:S(2)}) copy-start(bf16[256,192]{0,1:T(8,128)(2,1)} %copy-done.5) | copy-start | bytes 294916
Sparse Core Ops, SparseCore 0:
  11.7 88.5 all-gather.3
  102.5 59.9 all-gather.5
  168.5 167.9 all-reduce.2
  341.4 82.6 all-gather.7
  434.0 166.8 all-reduce.4
  604.1 41.5 reduce-scatter.1
